TPU v7x, 768 devices: a whole 4x8x12 slice. The times are simulated.
768 devices in a mesh: wide: 32 (over x, y_lo, core), pair: 12 (over z), sub: 2 (over y_hi).
Axes of the slice: x: 4, y: 8 (y_hi: 2, y_lo: 4; y = y_hi * 4 + y_lo), z: 12, core: 2. Of those that a mesh axis runs over, the one named last changes fastest.
Arguments:
- orbitals: bfloat16 [6, 64, 160, 160], P(None, ('wide', 'sub')), may hold values from -0.5 to 0.5
- couplings: bfloat16 [24, 160, 160], P('pair'), may hold values from -6 to 6
- blocks: int32 [24, 2], P('pair'), may hold values from 0 to 5, as said below
- partner: int32 [24], P('pair'), may hold values from 0 to 23, as said below
Outputs:
- self_energy: bfloat16 [24, 64, 160, 160], P('pair', ('wide', 'sub'))
Inputs may be any that keep to these rules, and one draw needn't show every extreme that they name: blocks[partner[b]] is blocks[b] with its two entries swapped, and the two entries of a row differ. partner is an involution without fixed points; the partner of a block lies among the 2 blocks of the index of pair that is half the pair axis away.
All inputs are finite; a program needn't handle non-finite values.
Results may differ from a plain program's by a relative error of at most 0.014.
Values may be sent and summed in bfloat16 or wider, within the bound.
No kernel may reach another device: no remote copies, remote signals or barrier semaphores. Data moves between devices by JAX's collectives and lax.ppermute only.
A program may use at most 32 MiB of HBM per device.

v0:
```python
import math

import jax
import jax.numpy as jnp
from jax import lax
from jax.sharding import PartitionSpec as P


def from_behind(value, axis, by):
    devices = lax.axis_size(axis)
    return lax.ppermute(value, axis, [(i, (i + by) % devices) for i in range(devices)])


def cut_along(value, dim, devices):
    before, after = (value.shape[:dim], value.shape[dim + 1 :])
    return jnp.moveaxis(value.reshape(*before, devices, -1, *after), dim, 0)


def in_order(parts, dim):
    parts = jnp.moveaxis(parts, 0, dim)
    lengths = parts.shape
    return parts.reshape(*lengths[:dim], lengths[dim] * lengths[dim + 1], *lengths[dim + 2 :])


def joined_exchange(value, axis, axes, splits, concats):
    sizes = [lax.axis_size(a) for a in axes]
    parts = cut_along(value, splits[0], sizes[0])
    parts = jnp.moveaxis(cut_along(parts, splits[1] + 1, sizes[1]), 0, 1)
    inside = parts.shape[2:]
    parts = parts.reshape(-1, *inside)
    parts = lax.all_to_all(parts, axis, split_axis=0, concat_axis=0, tiled=True)
    parts = in_order(parts.reshape(*sizes, *inside), concats[0] + 1)
    return in_order(parts, concats[1])


def spectral_tables(energy_count):
    padded = 2 * energy_count
    freq_count = energy_count + 1
    times_col = jnp.arange(energy_count, dtype=jnp.int32)[:, None]
    freq_row = jnp.arange(freq_count, dtype=jnp.int32)[None, :]
    phase = times_col * freq_row % padded
    phase_angle = 2.0 * math.pi / padded * phase.astype(jnp.float32)
    forward = jnp.concatenate([jnp.cos(phase_angle), -jnp.sin(phase_angle)], 1)
    weight = (
        jnp.where((freq_row == 0) | (freq_row == energy_count), 1.0, 2.0).astype(jnp.float32)
        / padded
    )
    inverse = jnp.concatenate(
        [(jnp.cos(phase_angle) * weight).T, (-jnp.sin(phase_angle) * weight).T], 0
    )
    return (forward, inverse)


def convolve(by_element, energy_count):
    forward, inverse = spectral_tables(energy_count)
    forward_high = forward.astype(jnp.bfloat16)
    forward_rest = (forward - forward_high.astype(jnp.float32)).astype(jnp.bfloat16)
    freq_count = energy_count + 1
    spectra = jnp.einsum(
        "sbtk,tf->sbfk", by_element, forward_high, preferred_element_type=jnp.float32
    )
    spectra = spectra + jnp.einsum(
        "sbtk,tf->sbfk", by_element, forward_rest, preferred_element_type=jnp.float32
    )
    first_real = spectra[0, :, :freq_count]
    first_imag = spectra[0, :, freq_count:]
    second_real = spectra[1, :, :freq_count]
    second_imag = spectra[1, :, freq_count:]
    prod_real = first_real * second_real - first_imag * second_imag
    prod_imag = first_real * second_imag + first_imag * second_real
    joined = jnp.concatenate([prod_real, prod_imag], 1)
    convolved = jnp.einsum("bfk,fe->bek", joined, inverse, precision=lax.Precision.HIGH)
    return (convolved * energy_count ** (-0.5)).astype(jnp.bfloat16)


def per_device(orbitals, couplings, blocks, partner):
    blk_count = couplings.shape[0]
    energy_local = orbitals.shape[1]
    block_order = orbitals.shape[2]
    left_side = jnp.take(orbitals, blocks[:, 0], axis=0)
    right_side = jnp.take(orbitals, blocks[:, 1], axis=0)
    inner_prod = jnp.einsum(
        "bemn,bnk->bemk", left_side, couplings, preferred_element_type=jnp.float32
    ).astype(jnp.bfloat16)
    direct = jnp.einsum(
        "bemk,benk->bemn", inner_prod, right_side, preferred_element_type=jnp.float32
    ).astype(jnp.bfloat16)
    half_axis = lax.axis_size("pair") // 2
    local_slot = partner % blk_count
    picker = (local_slot[:, None] == jnp.arange(blk_count, dtype=jnp.int32)[None, :]).astype(
        jnp.bfloat16
    )
    shifted = from_behind(couplings, "pair", half_axis)
    chosen = jnp.einsum("bk,kmn->bmn", picker, shifted, preferred_element_type=jnp.float32).astype(
        jnp.bfloat16
    )
    across = jnp.einsum(
        "benm,bmk->benk", right_side, chosen, preferred_element_type=jnp.float32
    ).astype(jnp.bfloat16)
    mirror = jnp.einsum(
        "bemk,benk->bemn", left_side, across, preferred_element_type=jnp.float32
    ).astype(jnp.bfloat16)
    stacked = jnp.stack([direct, mirror], 0)
    wide_count = lax.axis_size("wide")
    sub_count = lax.axis_size("sub")
    groups = wide_count * sub_count
    elem_count = block_order * block_order
    elem_piece = elem_count // groups
    energy_count = groups * energy_local
    outgoing = stacked.reshape(2, blk_count, 1, 1, energy_local, elem_count)
    incoming = joined_exchange(outgoing, ("wide", "sub"), ("wide", "sub"), (5, 5), (2, 3))
    by_element = incoming.reshape(2, blk_count, energy_count, elem_piece)
    polar = convolve(by_element, energy_count)
    returned = joined_exchange(
        polar.reshape(blk_count, wide_count, sub_count, energy_local, 1, 1, elem_piece),
        ("wide", "sub"),
        ("wide", "sub"),
        (1, 2),
        (4, 5),
    )
    polar_local = returned.reshape(blk_count, energy_local, block_order, block_order)
    screened = jnp.einsum(
        "bemn,benk->bemk", left_side, polar_local, preferred_element_type=jnp.float32
    ).astype(jnp.bfloat16)
    return jnp.einsum(
        "bemk,benk->bemn", screened, right_side, preferred_element_type=jnp.float32
    ).astype(jnp.bfloat16)


def solution(mesh):
    placed = (
        P(None, ("wide", "sub"), None, None),
        P("pair", None, None),
        P("pair", None),
        P("pair"),
    )
    return jax.shard_map(
        per_device,
        mesh=mesh,
        in_specs=placed,
        out_specs=P("pair", ("wide", "sub"), None, None),
        check_vma=False,
    )
```

profile of v0, /device:TPU:64, one launch (start us, length us, event | category | flops | bytes accessed | tf_op | source)
XLA Modules:
  0.0 71.7 jit_solution(14292390318997817195)
XLA Ops:
  0.0 1.1 %copy.10 = bf16[2,160,160]{2,0,1:T(2,128)(2,1)S(1)} copy(bf16[2,160,160]{2,1,0:T(8,128)(2,1)} %param.7) | data formatting | bytes 204800 | tf_op args[1]
  1.1 14.2 %collective-permute-start = (bf16[2,160,160]{2,0,1:T(2,128)(2,1)S(1)}, bf16[2,160,160]{2,0,1:T(2,128)(2,1)S(1)}, u32[]{:S(2)}, u32[]{:S(2)}) collective-permute-start(bf16[2,160,160]{2,0,1:T(2,128)(2,1)S(1)} %copy.10), channel_id=1, source_target_pairs={{0,12},{2,14},{4,16},{6,18},{8,20},{10,22},{12,0},{14,2},{16,4},{1... | collective-permute-start | bytes 307208 | tf_op jit(solution)/shard_map/ppermute | solution.py:11
  15.4 1.0 %slice_reduce_fusion = (s32[2]{0:T(128)S(1)}, s32[2]{0:T(128)S(1)}) fusion(s32[2,2]{1,0:T(2,128)} %param.8), kind=kLoop, calls=%fused_computation.76 | loop fusion | bytes 32 | tf_op jit(solution)/shard_map/slice | solution.py:81
  16.4 0.6 gather_fusion
  17.0 0.6 gather_fusion.1
  17.6 1.3 %convolution_convert_fusion.5 = bf16[2,160,160]{2,1,0:T(8,128)(2,1)S(1)} fusion(bf16[2,160,160]{2,1,0:T(8,128)(2,1)} %param.7, bf16[2,160,160]{2,1,0:T(8,128)(2,1)S(1)} %gather_fusion, pred[2]{0:T(512)(128)(4,1)S(1)} %get-tuple-element.17, bf16[2,160,160]{2,1,0:T(8,128)(2,1)S(1)} %gather_fusion.1, pred[2]{0:T(512)(128)(4,1)S(1)} %get-tuple-element.16), kind=kOutput, calls=%fused_computation.10 | convolution fusion | flops 32972800 | bytes 409604 | tf_op jit(solution)/shard_map/bemk,benk->bemn/dot_general | solution.py:85
  18.9 0.2 stack.9
  19.0 0.1 copy.12
  19.1 6.5 %collective-permute-done = bf16[2,160,160]{2,0,1:T(2,128)(2,1)S(1)} collective-permute-done((bf16[2,160,160]{2,0,1:T(2,128)(2,1)S(1)}, bf16[2,160,160]{2,0,1:T(2,128)(2,1)S(1)}, u32[]{:S(2)}, u32[]{:S(2)}) %collective-permute-start) | collective-permute-done | bytes 102432 | tf_op jit(solution)/shard_map/ppermute | solution.py:11
  25.7 0.4 convolution_convert_fusion
  26.1 0.4 convolution_convert_fusion.3
  26.5 0.2 stack.10
  26.7 0.1 copy.13
  26.8 0.3 maximum_bitcast_fusion
  27.1 0.3 fusion.52
  27.4 1.1 %pad_maximum_fusion = bf16[32,4,2,1,1,1,400]{6,2,1,0,5,4,3:T(2,128)(2,1)} fusion(bf16[32,2,2,1,1,1,400]{6,2,1,0,5,4,3:T(2,128)(2,1)S(1)} %get-tuple-element.11, bf16[32,2,2,1,1,1,400]{6,2,1,0,5,4,3:T(2,128)(2,1)S(1)} %get-tuple-element.10), kind=kLoop, calls=%fused_computation.20 | loop fusion | flops 102400 | bytes 409600 | tf_op jit(solution)/shard_map/concatenate
  28.4 10.6 %all-to-all-start = ((bf16[64,2,2,1,1,1,400]{6,2,1,5,4,3,0:T(2,128)(2,1)}), bf16[64,2,2,1,1,1,400]{6,2,1,5,4,3,0:T(2,128)(2,1)S(1)}, u32[]{:S(2)}, u32[]{:S(2)}) async-start(bf16[64,2,2,1,1,1,400]{6,2,1,5,4,3,0:T(2,128)(2,1)} %bitcast.12), calls=%async_computation | async-start | bytes 524288 | tf_op jit(solution)/shard_map/all_to_all | solution.py:31
  39.0 0.1 sine_negate_fusion
  39.2 0.2 cosine_multiply_fusion
  39.3 13.9 %all-to-all-done = bf16[64,2,2,1,1,1,400]{6,2,1,5,4,3,0:T(2,128)(2,1)S(1)} async-done(((bf16[64,2,2,1,1,1,400]{6,2,1,5,4,3,0:T(2,128)(2,1)}), bf16[64,2,2,1,1,1,400]{6,2,1,5,4,3,0:T(2,128)(2,1)S(1)}, u32[]{:S(2)}, u32[]{:S(2)}) %all-to-all-start) | async-done | bytes 204832 | tf_op jit(solution)/shard_map/all_to_all | solution.py:31
  53.2 0.2 copy.26
  53.4 0.2 reshape_reshape.8
  53.6 0.4 fusion.22
  54.0 0.4 fusion
  54.4 0.1 subtract_bitcast_fusion
  54.6 0.3 fusion.3
  54.9 0.1 reshape_reshape.9
  55.0 0.1 copy.16
  55.1 15.2 %all_to_all.10 = bf16[64,2,1,1,1,1,1,400]{7,1,6,5,4,3,2,0:T(2,128)(2,1)S(1)} all-to-all(bf16[64,2,1,1,1,1,1,400]{7,1,6,5,4,3,2,0:T(2,128)(2,1)S(1)} %bitcast.113), channel_id=1, replica_groups=mesh['wide'=32,'pair'=12,'sub'=2] {'wide','sub'}, dimensions={0} | all-to-all | bytes 204800 | tf_op jit(solution)/shard_map/all_to_all | solution.py:31
  70.3 0.1 copy.27
  70.5 0.2 reshape.104
  70.7 1.0 %fusion.2 = bf16[2,1,160,160]{3,2,1,0:T(8,128)(2,1)} fusion(bf16[2,160,160]{2,1,0:T(8,128)(2,1)S(1)} %reshape.104, bf16[2,160,160]{2,1,0:T(8,128)(2,1)S(1)} %gather_fusion, pred[2]{0:T(512)(128)(4,1)S(1)} %get-tuple-element.17, bf16[2,160,160]{2,1,0:T(8,128)(2,1)S(1)} %gather_fusion.1, pred[2]{0:T(512)(128)(4,1)S(1)} %get-tuple-element.16), kind=kOutput, calls=%fused_computation.13 | convolution fusion | flops 32972800 | bytes 409604 | tf_op jit(solution)/shard_map/bemk,benk->bemn/dot_general | solution.py:125
  (10 shorter events, 0.1 us)
Async XLA Ops:
  0.0 16.4 %copy-start = (bf16[6,1,160,160]{3,2,1,0:T(8,128)(2,1)S(1)}, bf16[6,1,160,160]{3,2,1,0:T(8,128)(2,1)}, u32[]{:S(2)}) copy-start(bf16[6,1,160,160]{3,2,1,0:T(8,128)(2,1)} %param.6) | copy-start | bytes 921604
  0.0 18.8 %copy-start.1 = (s32[2]{0:T(128)S(1)}, s32[2]{0:T(128)}, u32[]{:S(2)}) copy-start(s32[2]{0:T(128)} %param.9) | copy-start | bytes 28
  1.1 24.5 %collective-permute-start = (bf16[2,160,160]{2,0,1:T(2,128)(2,1)S(1)}, bf16[2,160,160]{2,0,1:T(2,128)(2,1)S(1)}, u32[]{:S(2)}, u32[]{:S(2)}) collective-permute-start(bf16[2,160,160]{2,0,1:T(2,128)(2,1)S(1)} %copy.10), channel_id=1, source_target_pairs={{0,12},{2,14},{4,16},{6,18},{8,20},{10,22},{12,0},{14,2},{16,4},{1... | collective-permute-start | bytes 307208 | tf_op jit(solution)/shard_map/ppermute | solution.py:11
  28.4 24.8 %all-to-all-start = ((bf16[64,2,2,1,1,1,400]{6,2,1,5,4,3,0:T(2,128)(2,1)}), bf16[64,2,2,1,1,1,400]{6,2,1,5,4,3,0:T(2,128)(2,1)S(1)}, u32[]{:S(2)}, u32[]{:S(2)}) async-start(bf16[64,2,2,1,1,1,400]{6,2,1,5,4,3,0:T(2,128)(2,1)} %bitcast.12), calls=%async_computation | async-start | bytes 524288 | tf_op jit(solution)/shard_map/all_to_all | solution.py:31
where the time goes:
time: 72 us; the launch traced here: 71.7 us
  starting transfers between devices  24.8 us (34%)
  waiting for transfers between devices  20.4 us (28%)
  blocking collectives  15.2 us (21%)
  local copies, waits for them, and re-layouts  4.98 us (7%)
  matrix products  4.23 us (6%)
  other arithmetic  1.84 us (3%)
    all_to_all x1, blocking collectives, joined_exchange(): parts = lax.all_to_all(parts, axis, split_axis=0, concat_axis=0, tiled=True)  15.2 us
    ppermute x1, starting transfers between devices, from_behind(): lax.ppermute(value, axis, [(i, (i + by) % devices) for i in range(devices)])  14.2 us
    all_to_all x1, waiting for transfers between devices, joined_exchange(): parts = lax.all_to_all(parts, axis, split_axis=0, concat_axis=0, tiled=True)  13.9 us
    all_to_all x1, starting transfers between devices, joined_exchange(): parts = lax.all_to_all(parts, axis, split_axis=0, concat_axis=0, tiled=True)  10.6 us
    ppermute x1, waiting for transfers between devices, from_behind(): lax.ppermute(value, axis, [(i, (i + by) % devices) for i in range(devices)])  6.53 us
  transfers between devices with their start and end apart: 2, of which 2 were waited for; matrix products, arithmetic and copies ran while one was open for 6% of the time, Pallas kernels for 0%

commit v1 on v0

v1 whole, which is shorter than its diff:
```python
import functools

import jax
import jax.numpy as jnp
from jax import lax
from jax.experimental import pallas as pl
from jax.experimental.pallas import tpu as pltpu
from jax.sharding import PartitionSpec as P

LANES = 128
ROWS = 8
VMEM = pl.BlockSpec(memory_space=pltpu.VMEM)
SMEM = pl.BlockSpec(memory_space=pltpu.SMEM)


def matmul(left, right):
    return jnp.dot(left, right, preferred_element_type=jnp.float32)


def matmul_t(left, right):
    return lax.dot_general(
        left, right, (((1,), (1,)), ((), ())), preferred_element_type=jnp.float32
    )


def pack(first, second):
    half = first.shape[0] // 2
    rest = jnp.concatenate(
        [
            first[:half, LANES:],
            first[half:, LANES:],
            second[:half, LANES:],
            second[half:, LANES:],
        ],
        axis=1,
    )
    return jnp.concatenate([first[:, :LANES], second[:, :LANES], rest], axis=0)


def direct_kernel(blocks, orbitals, couplings, out):
    results = []
    for b in range(2):
        left = orbitals[blocks[b, 0]]
        right = orbitals[blocks[b, 1]]
        inner = matmul(left, couplings[b]).astype(jnp.bfloat16)
        results.append(matmul_t(inner, right))
    out[...] = pack(*results).astype(jnp.bfloat16)


def mirror_kernel(blocks, partner, orbitals, shifted, direct, out):
    results = []
    for b in range(2):
        left = orbitals[blocks[b, 0]]
        right = orbitals[blocks[b, 1]]
        across = matmul(right, shifted[lax.rem(partner[b], 2)]).astype(jnp.bfloat16)
        results.append(matmul_t(left, across))
    mirror = pack(*results)
    used = direct.shape[0] // ROWS
    both = jnp.concatenate(
        [
            direct[...].astype(jnp.float32).reshape(used, ROWS, LANES),
            mirror.reshape(used, ROWS, LANES),
        ],
        axis=1,
    )
    out[:used] = both.astype(jnp.bfloat16)
    out[used:] = jnp.zeros((out.shape[0] - used, 2 * ROWS, LANES), jnp.bfloat16)


def convolve_kernel(tile, incoming, out, first, second):
    count = incoming.shape[0]
    both = incoming[...].astype(jnp.float32)
    first[...] = both[:, :ROWS]
    second[...] = both[:, ROWS:]
    scale = count ** (-0.5)
    for e0 in range(0, count, tile):
        totals = [None] * tile
        for t0 in range(0, e0 + tile, tile):
            lhs = [first[t0 + k] for k in range(tile)]
            base = e0 - t0 - tile + 1
            rhs = [
                second[base + k] if base + k >= 0 else None for k in range(2 * tile - 1)
            ]
            for de in range(tile):
                for dt in range(tile):
                    other = rhs[de - dt + tile - 1]
                    if other is None:
                        continue
                    term = lhs[dt] * other
                    totals[de] = term if totals[de] is None else totals[de] + term
        for de in range(0, tile, 2):
            pair = jnp.concatenate([totals[de], totals[de + 1]], axis=0) * scale
            out[pl.ds((e0 + de) * ROWS, 2 * ROWS), :] = pair.astype(jnp.bfloat16)


def screen_kernel(blocks, orbitals, packed, out):
    order = out.shape[1]
    half = order // 2
    rest = packed[2 * order : 2 * order + half, :]
    width = order - LANES
    for b in range(2):
        left = orbitals[blocks[b, 0]]
        right = orbitals[blocks[b, 1]]
        at = 2 * b * width
        tail = jnp.concatenate(
            [rest[:, at : at + width], rest[:, at + width : at + 2 * width]], axis=0
        )
        polar = jnp.concatenate([packed[b * order : (b + 1) * order, :], tail], axis=1)
        screened = matmul(left, polar).astype(jnp.bfloat16)
        out[b] = matmul_t(screened, right).astype(jnp.bfloat16)


def per_device(orbitals, couplings, blocks, partner):
    axes = ("wide", "sub")
    energies = lax.axis_size("wide") * lax.axis_size("sub")
    pairs = lax.axis_size("pair")
    order = couplings.shape[1]
    packed_rows = 2 * order * order // LANES
    shifted = lax.ppermute(
        couplings, "pair", [(i, (i + pairs // 2) % pairs) for i in range(pairs)]
    )
    sites = orbitals.reshape(orbitals.shape[0], order, order)
    direct = pl.pallas_call(
        direct_kernel,
        out_shape=jax.ShapeDtypeStruct((packed_rows, LANES), jnp.bfloat16),
        in_specs=[SMEM, VMEM, VMEM],
        out_specs=VMEM,
        name="direct",
    )(blocks, sites, couplings)
    outgoing = pl.pallas_call(
        mirror_kernel,
        out_shape=jax.ShapeDtypeStruct((energies, 2 * ROWS, LANES), jnp.bfloat16),
        in_specs=[SMEM, SMEM, VMEM, VMEM, VMEM],
        out_specs=VMEM,
        name="mirror",
    )(blocks, partner, sites, shifted, direct)
    incoming = lax.all_to_all(outgoing, axes, split_axis=0, concat_axis=0, tiled=True)
    polar = pl.pallas_call(
        functools.partial(convolve_kernel, 8),
        out_shape=jax.ShapeDtypeStruct((energies * ROWS, LANES), jnp.bfloat16),
        in_specs=[VMEM],
        out_specs=VMEM,
        scratch_shapes=[pltpu.VMEM((energies, ROWS, LANES), jnp.float32)] * 2,
        name="convolve",
    )(incoming)
    returned = lax.all_to_all(
        polar.reshape(energies, ROWS, LANES), axes, split_axis=0, concat_axis=0, tiled=True
    )
    result = pl.pallas_call(
        screen_kernel,
        out_shape=jax.ShapeDtypeStruct(couplings.shape, jnp.bfloat16),
        in_specs=[SMEM, VMEM, VMEM],
        out_specs=VMEM,
        name="screen",
    )(blocks, sites, returned.reshape(energies * ROWS, LANES))
    return result.reshape(couplings.shape[0], 1, order, order)


def solution(mesh):
    placed = (
        P(None, ("wide", "sub"), None, None),
        P("pair", None, None),
        P("pair", None),
        P("pair"),
    )
    return jax.shard_map(
        per_device,
        mesh=mesh,
        in_specs=placed,
        out_specs=P("pair", ("wide", "sub"), None, None),
        check_vma=False,
    )
```

time: 72 us -> 74 us (1.028)
  blocking collectives: 15.2 us -> 41.6 us
  waiting for transfers between devices: 20.4 us -> 8.36 us
  starting transfers between devices: 24.8 us -> 14.2 us
  Pallas kernels: 0 us -> 8.75 us
  local copies, waits for them, and re-layouts: 4.98 us -> 0.67 us
  matrix products: 4.23 us -> 0 us
  other arithmetic: 1.84 us -> 0 us
    all_to_all x1 -> x2, blocking collectives: 15.2 us -> 41.6 us  [the longest x1 24.9 us: per_device(): lax.all_to_all(outgoing, axes, split_axis=0, concat_axis=0, tiled=True)]
    all_to_all x1 -> x0, waiting for transfers between devices: 13.9 us -> none  [joined_exchange(): parts = lax.all_to_all(parts, axis, split_axis=0, concat_axis=0, tiled=True)]
    all_to_all x1 -> x0, starting transfers between devices: 10.6 us -> none  [joined_exchange(): parts = lax.all_to_all(parts, axis, split_axis=0, concat_axis=0, tiled=True)]
    pallas_call x0 -> x4, Pallas kernels: none -> 8.75 us  [the longest x1 2.28 us: per_device(): pl.pallas_call(mirror_kernel, out_shape=jax.ShapeDtypeStruct((energies, 2...]
    dot_general x7 -> x0, matrix products: 4.23 us -> none  [the longest x1 1.28 us: per_device(): jnp.einsum('bemk,benk->bemn', inner_prod, right_side, preferred_element_t...]
    ppermute x1, waiting for transfers between devices: 6.53 us -> 8.36 us  [per_device(): lax.ppermute(couplings, 'pair', [(i, (i + pairs // 2) % pairs) for i in r...]
    slice x2 -> x0, local copies, waits for them, and re-layouts: 1.25 us -> none  [the longest x1 0.97 us: per_device(): right_side = jnp.take(orbitals, blocks[:, 1], axis=0)]
    another operation x8 -> x0, local copies, waits for them, and re-layouts: 1.16 us -> none  [the longest x4 0.54 us: per_device(): stacked = jnp.stack([direct, mirror], 0)]
  transfers between devices with their start and end apart: 2 -> 1, of which waited for: 2 -> 1; matrix products, arithmetic and copies ran while one was open for 6% -> 0% of each run, Pallas kernels for 0% -> 3%
where the time goes in v1:
time: 74 us; the launch traced here: 73.6 us
  blocking collectives  41.6 us (56%)
  starting transfers between devices  14.2 us (19%)
  Pallas kernels  8.75 us (12%)
  waiting for transfers between devices  8.36 us (11%)
    all_to_all x1, blocking collectives, per_device(): lax.all_to_all(outgoing, axes, split_axis=0, concat_axis=0, tiled=True)  24.9 us
    all_to_all x1, blocking collectives, per_device(): lax.all_to_all(polar.reshape(energies, ROWS, LANES), axes, split_axis=0,...  16.8 us
    ppermute x1, starting transfers between devices, per_device(): lax.ppermute(couplings, 'pair', [(i, (i + pairs // 2) % pairs) for i in r...  14.2 us
    ppermute x1, waiting for transfers between devices, per_device(): lax.ppermute(couplings, 'pair', [(i, (i + pairs // 2) % pairs) for i in r...  8.36 us
    pallas_call x1, Pallas kernels, per_device(): pl.pallas_call(mirror_kernel, out_shape=jax.ShapeDtypeStruct((energies, 2...  2.28 us
    pallas_call x1, Pallas kernels, per_device(): pl.pallas_call(functools.partial(convolve_kernel, 8), out_shape=jax.Shape...  2.19 us
    pallas_call x1, Pallas kernels, per_device(): pl.pallas_call(screen_kernel, out_shape=jax.ShapeDtypeStruct(couplings.sh...  2.15 us
    pallas_call x1, Pallas kernels, per_device(): pl.pallas_call(direct_kernel, out_shape=jax.ShapeDtypeStruct((packed_rows...  2.13 us
  transfers between devices with their start and end apart: 1, of which 1 were waited for; matrix products, arithmetic and copies ran while one was open for 0% of the time, Pallas kernels for 3%

profile of v1, /device:TPU:64, one launch (start us, length us, event | category | flops | bytes accessed | tf_op | source)
XLA Modules:
  0.0 73.6 jit_solution(10643889749791939693)
XLA Ops:
  0.0 14.2 %collective-permute-start = (bf16[2,160,160]{2,1,0:T(8,128)(2,1)}, bf16[2,160,160]{2,1,0:T(8,128)(2,1)S(1)}, u32[]{:S(2)}, u32[]{:S(2)}) collective-permute-start(bf16[2,160,160]{2,1,0:T(8,128)(2,1)} %couplings.1), channel_id=1, source_target_pairs={{0,12},{2,14},{4,16},{6,18},{8,20},{10,22},{12,0},{14,2},{16,4},{1... | collective-permute-start | bytes 307208 | tf_op jit(solution)/shard_map/ppermute | solution.py:119
  14.2 2.1 %direct.1 = bf16[400,128]{1,0:T(8,128)(2,1)} custom-call(s32[2,2]{1,0:T(2,128)} %blocks.5, bf16[6,160,160]{2,1,0:T(8,128)(2,1)} %bitcast.6, bf16[2,160,160]{2,1,0:T(8,128)(2,1)} %couplings.1), custom_call_target="tpu_custom_call" | custom-call | tf_op jit(solution)/shard_map/direct/pallas_call | solution.py:123
  16.4 8.4 %collective-permute-done.shifted = bf16[2,160,160]{2,1,0:T(8,128)(2,1)S(1)} collective-permute-done((bf16[2,160,160]{2,1,0:T(8,128)(2,1)}, bf16[2,160,160]{2,1,0:T(8,128)(2,1)S(1)}, u32[]{:S(2)}, u32[]{:S(2)}) %collective-permute-start) | collective-permute-done | bytes 102432 | tf_op jit(solution)/shard_map/ppermute | solution.py:119
  24.7 0.0 copy-start
  24.7 0.7 copy-done
  25.4 2.3 %mirror.1 = bf16[64,16,128]{2,1,0:T(8,128)(2,1)} custom-call(s32[2,2]{1,0:T(2,128)} %blocks.5, s32[2]{0:T(128)} %partner.1, bf16[6,160,160]{2,1,0:T(8,128)(2,1)} %bitcast.7, bf16[2,160,160]{2,1,0:T(8,128)(2,1)} %copy-done, bf16[400,128]{1,0:T(8,128)(2,1)} %direct.1), custom_call_target="tpu_custom_call" | custom-call | tf_op jit(solution)/shard_map/mirror/pallas_call | solution.py:130
  27.7 24.9 %all_to_all.10.incoming = bf16[64,16,128]{2,1,0:T(8,128)(2,1)} all-to-all(bf16[64,16,128]{2,1,0:T(8,128)(2,1)} %mirror.1), channel_id=1, replica_groups=mesh['wide'=32,'pair'=12,'sub'=2] {'wide','sub'}, dimensions={0} | all-to-all | bytes 524288 | tf_op jit(solution)/shard_map/all_to_all | solution.py:137
  52.5 2.2 %convolve.1 = bf16[512,128]{1,0:T(8,128)(2,1)} custom-call(bf16[64,16,128]{2,1,0:T(8,128)(2,1)} %all_to_all.10.incoming), custom_call_target="tpu_custom_call" | custom-call | tf_op jit(solution)/shard_map/convolve/pallas_call | solution.py:138
  54.7 16.8 %all_to_all.11 = bf16[64,8,128]{2,1,0:T(8,128)(2,1)} all-to-all(bf16[64,8,128]{2,1,0:T(8,128)(2,1)} %bitcast.9), channel_id=1, replica_groups=mesh['wide'=32,'pair'=12,'sub'=2] {'wide','sub'}, dimensions={0} | all-to-all | bytes 262144 | tf_op jit(solution)/shard_map/all_to_all | solution.py:146
  71.5 2.1 %screen.1 = bf16[2,160,160]{2,1,0:T(8,128)(2,1)} custom-call(s32[2,2]{1,0:T(2,128)} %blocks.5, bf16[6,160,160]{2,1,0:T(8,128)(2,1)} %bitcast.8, bf16[512,128]{1,0:T(8,128)(2,1)} %bitcast.10), custom_call_target="tpu_custom_call" | custom-call | tf_op jit(solution)/shard_map/screen/pallas_call | solution.py:149
Async XLA Ops:
  0.0 24.7 %collective-permute-start = (bf16[2,160,160]{2,1,0:T(8,128)(2,1)}, bf16[2,160,160]{2,1,0:T(8,128)(2,1)S(1)}, u32[]{:S(2)}, u32[]{:S(2)}) collective-permute-start(bf16[2,160,160]{2,1,0:T(8,128)(2,1)} %couplings.1), channel_id=1, source_target_pairs={{0,12},{2,14},{4,16},{6,18},{8,20},{10,22},{12,0},{14,2},{16,4},{1... | collective-permute-start | bytes 307208 | tf_op jit(solution)/shard_map/ppermute | solution.py:119
  24.7 0.7 copy-start

commit v2 on v1

--- a/solution.py
+++ b/solution.py
@@ -110,6 +110,10 @@
         out[b] = matmul_t(screened, right).astype(jnp.bfloat16)
 
 
+def onchip(value):
+    return pltpu.with_memory_space_constraint(value, pltpu.VMEM)
+
+
 def per_device(orbitals, couplings, blocks, partner):
     axes = ("wide", "sub")
     energies = lax.axis_size("wide") * lax.axis_size("sub")
@@ -119,30 +123,31 @@
     shifted = lax.ppermute(
         couplings, "pair", [(i, (i + pairs // 2) % pairs) for i in range(pairs)]
     )
-    sites = orbitals.reshape(orbitals.shape[0], order, order)
+    sites = onchip(orbitals.reshape(orbitals.shape[0], order, order))
+    here = onchip(couplings)
     direct = pl.pallas_call(
         direct_kernel,
-        out_shape=jax.ShapeDtypeStruct((packed_rows, LANES), jnp.bfloat16),
+        out_shape=pltpu.VMEM((packed_rows, LANES), jnp.bfloat16),
         in_specs=[SMEM, VMEM, VMEM],
         out_specs=VMEM,
         name="direct",
-    )(blocks, sites, couplings)
+    )(blocks, sites, here)
     outgoing = pl.pallas_call(
         mirror_kernel,
-        out_shape=jax.ShapeDtypeStruct((energies, 2 * ROWS, LANES), jnp.bfloat16),
+        out_shape=pltpu.VMEM((energies, 2 * ROWS, LANES), jnp.bfloat16),
         in_specs=[SMEM, SMEM, VMEM, VMEM, VMEM],
         out_specs=VMEM,
         name="mirror",
-    )(blocks, partner, sites, shifted, direct)
+    )(blocks, partner, sites, onchip(shifted), onchip(direct))
     incoming = lax.all_to_all(outgoing, axes, split_axis=0, concat_axis=0, tiled=True)
     polar = pl.pallas_call(
         functools.partial(convolve_kernel, 8),
-        out_shape=jax.ShapeDtypeStruct((energies * ROWS, LANES), jnp.bfloat16),
+        out_shape=pltpu.VMEM((energies * ROWS, LANES), jnp.bfloat16),
         in_specs=[VMEM],
         out_specs=VMEM,
         scratch_shapes=[pltpu.VMEM((energies, ROWS, LANES), jnp.float32)] * 2,
         name="convolve",
-    )(incoming)
+    )(onchip(incoming))
     returned = lax.all_to_all(
         polar.reshape(energies, ROWS, LANES), axes, split_axis=0, concat_axis=0, tiled=True
     )
@@ -152,7 +157,7 @@
         in_specs=[SMEM, VMEM, VMEM],
         out_specs=VMEM,
         name="screen",
-    )(blocks, sites, returned.reshape(energies * ROWS, LANES))
+    )(blocks, sites, onchip(returned.reshape(energies * ROWS, LANES)))
     return result.reshape(couplings.shape[0], 1, order, order)
 
 

time: 74 us -> 68.5 us (0.926)
  Pallas kernels: 8.75 us -> 4.59 us
  blocking collectives: 41.6 us -> 39.9 us
  local copies, waits for them, and re-layouts: 0.67 us -> 1.95 us
  waiting for transfers between devices: 8.36 us -> 7.45 us
    pallas_call x3, Pallas kernels: 6.6 us -> 2.82 us  [the longest x1 1.13 us: per_device(): pl.pallas_call(mirror_kernel, out_shape=pltpu.VMEM((energies, 2 * ROWS, L...]
    all_to_all x1, blocking collectives: 16.8 us -> 15.2 us  [per_device(): lax.all_to_all(polar.reshape(energies, ROWS, LANES), axes, split_axis=0,...]
    unnamed x2 -> x6, local copies, waits for them, and re-layouts: 0.67 us -> 1.95 us
    ppermute x1, waiting for transfers between devices: 8.36 us -> 7.45 us  [per_device(): lax.ppermute(couplings, 'pair', [(i, (i + pairs // 2) % pairs) for i in r...]
  transfers between devices with their start and end apart: 1 -> 1, of which waited for: 1 -> 1; matrix products, arithmetic and copies ran while one was open for 0% -> 0% of each run, Pallas kernels for 3% -> 2%
where the time goes in v2:
time: 68.5 us; the launch traced here: 68.2 us
  blocking collectives  39.9 us (58%)
  starting transfers between devices  14.2 us (21%)
  waiting for transfers between devices  7.45 us (11%)
  Pallas kernels  4.59 us (7%)
  local copies, waits for them, and re-layouts  1.95 us (3%)
    all_to_all x1, blocking collectives, per_device(): lax.all_to_all(outgoing, axes, split_axis=0, concat_axis=0, tiled=True)  24.7 us
    all_to_all x1, blocking collectives, per_device(): lax.all_to_all(polar.reshape(energies, ROWS, LANES), axes, split_axis=0,...  15.2 us
    ppermute x1, starting transfers between devices, per_device(): lax.ppermute(couplings, 'pair', [(i, (i + pairs // 2) % pairs) for i in r...  14.2 us
    ppermute x1, waiting for transfers between devices, per_device(): lax.ppermute(couplings, 'pair', [(i, (i + pairs // 2) % pairs) for i in r...  7.45 us
    unnamed x6, local copies, waits for them, and re-layouts  1.95 us
    pallas_call x1, Pallas kernels, per_device(): pl.pallas_call(screen_kernel, out_shape=jax.ShapeDtypeStruct(couplings.sh...  1.77 us
  transfers between devices with their start and end apart: 1, of which 1 were waited for; matrix products, arithmetic and copies ran while one was open for 0% of the time, Pallas kernels for 2%

profile of v2, /device:TPU:64, one launch (start us, length us, event | category | flops | bytes accessed | tf_op | source)
XLA Modules:
  0.0 68.2 jit_solution(16603716015980213666)
XLA Ops:
  0.0 14.2 %collective-permute-start = (bf16[2,160,160]{2,1,0:T(8,128)(2,1)}, bf16[2,160,160]{2,1,0:T(8,128)(2,1)S(1)}, u32[]{:S(2)}, u32[]{:S(2)}) collective-permute-start(bf16[2,160,160]{2,1,0:T(8,128)(2,1)} %couplings.1), channel_id=1, source_target_pairs={{0,12},{2,14},{4,16},{6,18},{8,20},{10,22},{12,0},{14,2},{16,4},{1... | collective-permute-start | bytes 307208 | tf_op jit(solution)/shard_map/ppermute | solution.py:123
  14.2 0.0 copy-start
  14.2 1.0 %copy-done = bf16[6,1,160,160]{3,2,1,0:T(8,128)(2,1)S(1)} copy-done((bf16[6,1,160,160]{3,2,1,0:T(8,128)(2,1)S(1)}, bf16[6,1,160,160]{3,2,1,0:T(8,128)(2,1)}, u32[]{:S(2)}) %copy-start) | copy-done | bytes 307224
  15.3 0.0 copy-start.2
  15.3 0.9 %copy-done.2 = bf16[2,160,160]{2,1,0:T(8,128)(2,1)S(1)} copy-done((bf16[2,160,160]{2,1,0:T(8,128)(2,1)S(1)}, bf16[2,160,160]{2,1,0:T(8,128)(2,1)}, u32[]{:S(2)}) %copy-start.2) | copy-done | bytes 102424
  16.2 1.1 %direct.1 = bf16[400,128]{1,0:T(8,128)(2,1)S(1)} custom-call(s32[2,2]{1,0:T(2,128)} %blocks.5, bf16[6,160,160]{2,1,0:T(8,128)(2,1)S(1)} %bitcast.6, bf16[2,160,160]{2,1,0:T(8,128)(2,1)S(1)} %copy-done.2), custom_call_target="tpu_custom_call" | custom-call | tf_op jit(solution)/shard_map/direct/pallas_call | solution.py:128
  17.3 7.4 %collective-permute-done.shifted = bf16[2,160,160]{2,1,0:T(8,128)(2,1)S(1)} collective-permute-done((bf16[2,160,160]{2,1,0:T(8,128)(2,1)}, bf16[2,160,160]{2,1,0:T(8,128)(2,1)S(1)}, u32[]{:S(2)}, u32[]{:S(2)}) %collective-permute-start) | collective-permute-done | bytes 102432 | tf_op jit(solution)/shard_map/ppermute | solution.py:123
  24.7 1.1 %mirror.1 = bf16[64,16,128]{2,1,0:T(8,128)(2,1)S(1)} custom-call(s32[2,2]{1,0:T(2,128)} %blocks.5, s32[2]{0:T(128)} %partner.1, bf16[6,160,160]{2,1,0:T(8,128)(2,1)S(1)} %bitcast.7, bf16[2,160,160]{2,1,0:T(8,128)(2,1)S(1)} %collective-permute-done.shifted, bf16[400,128]{1,0:T(8,128)(2,1)S(1)} %direct.1), custom_call_target="tpu_custom_call" | custom-call | tf_op jit(solution)/shard_map/mirror/pallas_call | solution.py:135
  25.9 0.0 copy-start.1
  25.9 24.7 %all_to_all.10.incoming = bf16[64,16,128]{2,1,0:T(8,128)(2,1)S(1)} all-to-all(bf16[64,16,128]{2,1,0:T(8,128)(2,1)S(1)} %mirror.1), channel_id=1, replica_groups=mesh['wide'=32,'pair'=12,'sub'=2] {'wide','sub'}, dimensions={0} | all-to-all | bytes 524288 | tf_op jit(solution)/shard_map/all_to_all | solution.py:142
  50.6 0.6 convolve.1
  51.2 15.2 %all_to_all.11 = bf16[64,8,128]{2,1,0:T(8,128)(2,1)S(1)} all-to-all(bf16[64,8,128]{2,1,0:T(8,128)(2,1)S(1)} %bitcast.9), channel_id=1, replica_groups=mesh['wide'=32,'pair'=12,'sub'=2] {'wide','sub'}, dimensions={0} | all-to-all | bytes 262144 | tf_op jit(solution)/shard_map/all_to_all | solution.py:151
  66.4 0.0 copy-done.1
  66.4 1.8 %screen.1 = bf16[2,160,160]{2,1,0:T(8,128)(2,1)} custom-call(s32[2,2]{1,0:T(2,128)} %blocks.5, bf16[6,160,160]{2,1,0:T(8,128)(2,1)S(1)} %bitcast.8, bf16[512,128]{1,0:T(8,128)(2,1)S(1)} %bitcast.10), custom_call_target="tpu_custom_call" | custom-call | tf_op jit(solution)/shard_map/screen/pallas_call | solution.py:154
Async XLA Ops:
  0.0 24.7 %collective-permute-start = (bf16[2,160,160]{2,1,0:T(8,128)(2,1)}, bf16[2,160,160]{2,1,0:T(8,128)(2,1)S(1)}, u32[]{:S(2)}, u32[]{:S(2)}) collective-permute-start(bf16[2,160,160]{2,1,0:T(8,128)(2,1)} %couplings.1), channel_id=1, source_target_pairs={{0,12},{2,14},{4,16},{6,18},{8,20},{10,22},{12,0},{14,2},{16,4},{1... | collective-permute-start | bytes 307208 | tf_op jit(solution)/shard_map/ppermute | solution.py:123
  14.2 1.0 %copy-start = (bf16[6,1,160,160]{3,2,1,0:T(8,128)(2,1)S(1)}, bf16[6,1,160,160]{3,2,1,0:T(8,128)(2,1)}, u32[]{:S(2)}) copy-start(bf16[6,1,160,160]{3,2,1,0:T(8,128)(2,1)} %param.4) | copy-start | bytes 921604
  15.3 0.9 %copy-start.2 = (bf16[2,160,160]{2,1,0:T(8,128)(2,1)S(1)}, bf16[2,160,160]{2,1,0:T(8,128)(2,1)}, u32[]{:S(2)}) copy-start(bf16[2,160,160]{2,1,0:T(8,128)(2,1)} %couplings.1) | copy-start | bytes 307204
  25.9 40.5 %copy-start.1 = (bf16[6,1,160,160]{3,2,1,0:T(8,128)(2,1)S(1)}, bf16[6,1,160,160]{3,2,1,0:T(8,128)(2,1)}, u32[]{:S(2)}) copy-start(bf16[6,1,160,160]{3,2,1,0:T(8,128)(2,1)} %param.4) | copy-start | bytes 921604

commit v3 on v2

--- a/solution.py
+++ b/solution.py
@@ -5,6 +5,7 @@
 from jax import lax
 from jax.experimental import pallas as pl
 from jax.experimental.pallas import tpu as pltpu
+from jax.sharding import Mesh
 from jax.sharding import PartitionSpec as P
 
 LANES = 128
@@ -37,41 +38,33 @@
     return jnp.concatenate([first[:, :LANES], second[:, :LANES], rest], axis=0)
 
 
-def direct_kernel(blocks, orbitals, couplings, out):
+def direct_kernel(total, blocks, partner, orbitals, couplings, out, inner):
+    groups = out.shape[0] // 2
+    used = 2 * couplings.shape[1] * couplings.shape[2] // (ROWS * LANES)
+    low = lax.select(partner[0] < total // 2, 1, 0)
     results = []
     for b in range(2):
         left = orbitals[blocks[b, 0]]
         right = orbitals[blocks[b, 1]]
-        inner = matmul(left, couplings[b]).astype(jnp.bfloat16)
-        results.append(matmul_t(inner, right))
-    out[...] = pack(*results).astype(jnp.bfloat16)
-
-
-def mirror_kernel(blocks, partner, orbitals, shifted, direct, out):
+        inner[b] = matmul(left, couplings[b]).astype(jnp.bfloat16)
+        results.append(matmul_t(inner[b], right))
+    flat = pack(*results).astype(jnp.bfloat16)
+    out[pl.ds(low * groups, used)] = flat.reshape(used, ROWS, LANES)
+    first = lax.rem(partner[0], 2)
     results = []
-    for b in range(2):
-        left = orbitals[blocks[b, 0]]
-        right = orbitals[blocks[b, 1]]
-        across = matmul(right, shifted[lax.rem(partner[b], 2)]).astype(jnp.bfloat16)
-        results.append(matmul_t(left, across))
-    mirror = pack(*results)
-    used = direct.shape[0] // ROWS
-    both = jnp.concatenate(
-        [
-            direct[...].astype(jnp.float32).reshape(used, ROWS, LANES),
-            mirror.reshape(used, ROWS, LANES),
-        ],
-        axis=1,
-    )
-    out[:used] = both.astype(jnp.bfloat16)
-    out[used:] = jnp.zeros((out.shape[0] - used, 2 * ROWS, LANES), jnp.bfloat16)
+    for b in (first, 1 - first):
+        results.append(matmul_t(orbitals[blocks[b, 1]], inner[b]))
+    flat = pack(*results).astype(jnp.bfloat16)
+    out[pl.ds((1 - low) * groups, used)] = flat.reshape(used, ROWS, LANES)
+    rest = jnp.zeros((groups - used, ROWS, LANES), jnp.bfloat16)
+    out[used:groups] = rest
+    out[groups + used :] = rest
 
 
 def convolve_kernel(tile, incoming, out, first, second):
-    count = incoming.shape[0]
-    both = incoming[...].astype(jnp.float32)
-    first[...] = both[:, :ROWS]
-    second[...] = both[:, ROWS:]
+    count = incoming.shape[0] // 2
+    first[...] = incoming[:count].astype(jnp.float32)
+    second[...] = incoming[count:].astype(jnp.float32)
     scale = count ** (-0.5)
     for e0 in range(0, count, tile):
         totals = [None] * tile
@@ -114,32 +107,22 @@
     return pltpu.with_memory_space_constraint(value, pltpu.VMEM)
 
 
-def per_device(orbitals, couplings, blocks, partner):
+def per_device(total, orbitals, couplings, blocks, partner):
     axes = ("wide", "sub")
     energies = lax.axis_size("wide") * lax.axis_size("sub")
-    pairs = lax.axis_size("pair")
     order = couplings.shape[1]
-    packed_rows = 2 * order * order // LANES
-    shifted = lax.ppermute(
-        couplings, "pair", [(i, (i + pairs // 2) % pairs) for i in range(pairs)]
+    sites = onchip(orbitals.reshape(orbitals.shape[0], order, order))
+    outgoing = pl.pallas_call(
+        functools.partial(direct_kernel, total),
+        out_shape=pltpu.VMEM((2 * energies, ROWS, LANES), jnp.bfloat16),
+        in_specs=[SMEM, SMEM, VMEM, VMEM],
+        out_specs=VMEM,
+        scratch_shapes=[pltpu.VMEM(couplings.shape, jnp.bfloat16)],
+        name="direct",
+    )(blocks, partner, sites, onchip(couplings))
+    incoming = lax.all_to_all(
+        outgoing, ("half",) + axes, split_axis=0, concat_axis=0, tiled=True
     )
-    sites = onchip(orbitals.reshape(orbitals.shape[0], order, order))
-    here = onchip(couplings)
-    direct = pl.pallas_call(
-        direct_kernel,
-        out_shape=pltpu.VMEM((packed_rows, LANES), jnp.bfloat16),
-        in_specs=[SMEM, VMEM, VMEM],
-        out_specs=VMEM,
-        name="direct",
-    )(blocks, sites, here)
-    outgoing = pl.pallas_call(
-        mirror_kernel,
-        out_shape=pltpu.VMEM((energies, 2 * ROWS, LANES), jnp.bfloat16),
-        in_specs=[SMEM, SMEM, VMEM, VMEM, VMEM],
-        out_specs=VMEM,
-        name="mirror",
-    )(blocks, partner, sites, onchip(shifted), onchip(direct))
-    incoming = lax.all_to_all(outgoing, axes, split_axis=0, concat_axis=0, tiled=True)
     polar = pl.pallas_call(
         functools.partial(convolve_kernel, 8),
         out_shape=pltpu.VMEM((energies * ROWS, LANES), jnp.bfloat16),
@@ -162,16 +145,23 @@
 
 
 def solution(mesh):
+    sizes = mesh.shape
+    pairs = sizes["pair"]
+    halved = Mesh(
+        mesh.devices.reshape(sizes["wide"], 2, pairs // 2, sizes["sub"]),
+        ("wide", "half", "inside", "sub"),
+    )
+    pair = ("half", "inside")
     placed = (
         P(None, ("wide", "sub"), None, None),
-        P("pair", None, None),
-        P("pair", None),
-        P("pair"),
+        P(pair, None, None),
+        P(pair, None),
+        P(pair),
     )
     return jax.shard_map(
-        per_device,
-        mesh=mesh,
+        functools.partial(per_device, 2 * pairs),
+        mesh=halved,
         in_specs=placed,
-        out_specs=P("pair", ("wide", "sub"), None, None),
+        out_specs=P(pair, ("wide", "sub"), None, None),
         check_vma=False,
     )

time: 68.5 us -> 69.1 us (level)
  the two profiles are of different devices: /device:TPU:64 before, /device:TPU:1 now
where the time goes in v3:
time: 69.1 us; the launch traced here: 68.8 us
  blocking collectives  63.2 us (91%)
  Pallas kernels  3.6 us (5%)
  local copies, waits for them, and re-layouts  1.95 us (3%)
    all_to_all x1, blocking collectives, per_device(): lax.all_to_all(outgoing, ('half',) + axes, split_axis=0, concat_axis=0, t...  47.6 us
    all_to_all x1, blocking collectives, per_device(): lax.all_to_all(polar.reshape(energies, ROWS, LANES), axes, split_axis=0,...  15.6 us
    unnamed x6, local copies, waits for them, and re-layouts  1.95 us
    pallas_call x1, Pallas kernels, per_device(): pl.pallas_call(screen_kernel, out_shape=jax.ShapeDtypeStruct(couplings.sh...  1.77 us

profile of v3, /device:TPU:1, one launch (start us, length us, event | category | flops | bytes accessed | tf_op | source)
XLA Modules:
  0.0 68.8 jit_solution(14871114093317815326)
XLA Ops:
  0.0 0.0 copy-start
  0.0 1.0 %copy-done = bf16[6,1,160,160]{3,2,1,0:T(8,128)(2,1)S(1)} copy-done((bf16[6,1,160,160]{3,2,1,0:T(8,128)(2,1)S(1)}, bf16[6,1,160,160]{3,2,1,0:T(8,128)(2,1)}, u32[]{:S(2)}) %copy-start) | copy-done | bytes 307224
  1.0 0.0 copy-start.2
  1.0 0.9 %copy-done.2 = bf16[2,160,160]{2,1,0:T(8,128)(2,1)S(1)} copy-done((bf16[2,160,160]{2,1,0:T(8,128)(2,1)S(1)}, bf16[2,160,160]{2,1,0:T(8,128)(2,1)}, u32[]{:S(2)}) %copy-start.2) | copy-done | bytes 102424
  1.9 1.2 %direct.1 = bf16[128,8,128]{2,1,0:T(8,128)(2,1)S(1)} custom-call(s32[2,2]{1,0:T(2,128)} %blocks.3, s32[2]{0:T(128)} %partner.1, bf16[6,160,160]{2,1,0:T(8,128)(2,1)S(1)} %bitcast.6, bf16[2,160,160]{2,1,0:T(8,128)(2,1)S(1)} %copy-done.2), custom_call_target="tpu_custom_call" | custom-call | tf_op jit(solution)/shard_map/direct/pallas_call | solution.py:115
  3.2 0.0 copy-start.1
  3.2 47.6 %all_to_all.10.incoming = bf16[128,8,128]{2,1,0:T(8,128)(2,1)S(1)} all-to-all(bf16[128,8,128]{2,1,0:T(8,128)(2,1)S(1)} %direct.1), channel_id=1, replica_groups=mesh['wide'=32,'half'=2,'inside'=6,'sub'=2] {'half','wide','sub'}, dimensions={0} | all-to-all | bytes 524288 | tf_op jit(solution)/shard_map/all_to_all | solution.py:123
  50.8 0.6 convolve.1
  51.4 15.6 %all_to_all.11 = bf16[64,8,128]{2,1,0:T(8,128)(2,1)S(1)} all-to-all(bf16[64,8,128]{2,1,0:T(8,128)(2,1)S(1)} %bitcast.8), channel_id=1, replica_groups=mesh['wide'=32,'half'=2,'inside'=6,'sub'=2] {'wide','sub'}, dimensions={0} | all-to-all | bytes 262144 | tf_op jit(solution)/shard_map/all_to_all | solution.py:134
  67.0 0.0 copy-done.1
  67.0 1.8 %screen.1 = bf16[2,160,160]{2,1,0:T(8,128)(2,1)} custom-call(s32[2,2]{1,0:T(2,128)} %blocks.3, bf16[6,160,160]{2,1,0:T(8,128)(2,1)S(1)} %bitcast.7, bf16[512,128]{1,0:T(8,128)(2,1)S(1)} %bitcast.9), custom_call_target="tpu_custom_call" | custom-call | tf_op jit(solution)/shard_map/screen/pallas_call | solution.py:137
Async XLA Ops:
  0.0 1.0 %copy-start = (bf16[6,1,160,160]{3,2,1,0:T(8,128)(2,1)S(1)}, bf16[6,1,160,160]{3,2,1,0:T(8,128)(2,1)}, u32[]{:S(2)}) copy-start(bf16[6,1,160,160]{3,2,1,0:T(8,128)(2,1)} %param.4) | copy-start | bytes 921604
  1.0 0.9 %copy-start.2 = (bf16[2,160,160]{2,1,0:T(8,128)(2,1)S(1)}, bf16[2,160,160]{2,1,0:T(8,128)(2,1)}, u32[]{:S(2)}) copy-start(bf16[2,160,160]{2,1,0:T(8,128)(2,1)} %couplings.1) | copy-start | bytes 307204
  3.2 63.8 %copy-start.1 = (bf16[6,1,160,160]{3,2,1,0:T(8,128)(2,1)S(1)}, bf16[6,1,160,160]{3,2,1,0:T(8,128)(2,1)}, u32[]{:S(2)}) copy-start(bf16[6,1,160,160]{3,2,1,0:T(8,128)(2,1)} %param.4) | copy-start | bytes 921604

commit v4 on v2

--- a/solution.py
+++ b/solution.py
@@ -6,6 +6,7 @@
 from jax.experimental import pallas as pl
 from jax.experimental.pallas import tpu as pltpu
 from jax.sharding import PartitionSpec as P
+
 
 LANES = 128
 ROWS = 8
@@ -37,6 +38,13 @@
     return jnp.concatenate([first[:, :LANES], second[:, :LANES], rest], axis=0)
 
 
+def put(out, matrices):
+    flat = pack(*matrices).astype(jnp.bfloat16)
+    used = flat.shape[0] // ROWS
+    out[:used] = flat.reshape(used, ROWS, LANES)
+    out[used:] = jnp.zeros((out.shape[0] - used, ROWS, LANES), jnp.bfloat16)
+
+
 def direct_kernel(blocks, orbitals, couplings, out):
     results = []
     for b in range(2):
@@ -44,34 +52,26 @@
         right = orbitals[blocks[b, 1]]
         inner = matmul(left, couplings[b]).astype(jnp.bfloat16)
         results.append(matmul_t(inner, right))
-    out[...] = pack(*results).astype(jnp.bfloat16)
+    put(out, results)
 
 
-def mirror_kernel(blocks, partner, orbitals, shifted, direct, out):
+def mirror_kernel(blocks, partner, orbitals, shifted, out):
     results = []
     for b in range(2):
         left = orbitals[blocks[b, 0]]
         right = orbitals[blocks[b, 1]]
         across = matmul(right, shifted[lax.rem(partner[b], 2)]).astype(jnp.bfloat16)
         results.append(matmul_t(left, across))
-    mirror = pack(*results)
-    used = direct.shape[0] // ROWS
-    both = jnp.concatenate(
-        [
-            direct[...].astype(jnp.float32).reshape(used, ROWS, LANES),
-            mirror.reshape(used, ROWS, LANES),
-        ],
-        axis=1,
-    )
-    out[:used] = both.astype(jnp.bfloat16)
-    out[used:] = jnp.zeros((out.shape[0] - used, 2 * ROWS, LANES), jnp.bfloat16)
+    put(out, results)
 
 
-def convolve_kernel(tile, incoming, out, first, second):
-    count = incoming.shape[0]
-    both = incoming[...].astype(jnp.float32)
-    first[...] = both[:, :ROWS]
-    second[...] = both[:, ROWS:]
+def widen_kernel(value, out):
+    out[...] = value[...].astype(jnp.float32)
+
+
+def convolve_kernel(tile, first, mirror, out, second):
+    count = first.shape[0]
+    second[...] = mirror[...].astype(jnp.float32)
     scale = count ** (-0.5)
     for e0 in range(0, count, tile):
         totals = [None] * tile
@@ -119,38 +119,47 @@
     energies = lax.axis_size("wide") * lax.axis_size("sub")
     pairs = lax.axis_size("pair")
     order = couplings.shape[1]
-    packed_rows = 2 * order * order // LANES
+
+    def exchange(value):
+        return lax.all_to_all(value, axes, split_axis=0, concat_axis=0, tiled=True)
+
+    slots = pltpu.VMEM((energies, ROWS, LANES), jnp.bfloat16)
     shifted = lax.ppermute(
         couplings, "pair", [(i, (i + pairs // 2) % pairs) for i in range(pairs)]
     )
     sites = onchip(orbitals.reshape(orbitals.shape[0], order, order))
-    here = onchip(couplings)
     direct = pl.pallas_call(
         direct_kernel,
-        out_shape=pltpu.VMEM((packed_rows, LANES), jnp.bfloat16),
+        out_shape=slots,
         in_specs=[SMEM, VMEM, VMEM],
         out_specs=VMEM,
         name="direct",
-    )(blocks, sites, here)
-    outgoing = pl.pallas_call(
+    )(blocks, sites, onchip(couplings))
+    direct = exchange(direct)
+    direct = pl.pallas_call(
+        widen_kernel,
+        out_shape=pltpu.VMEM((energies, ROWS, LANES), jnp.float32),
+        in_specs=[VMEM],
+        out_specs=VMEM,
+        name="widen",
+    )(onchip(direct))
+    mirror = pl.pallas_call(
         mirror_kernel,
-        out_shape=pltpu.VMEM((energies, 2 * ROWS, LANES), jnp.bfloat16),
-        in_specs=[SMEM, SMEM, VMEM, VMEM, VMEM],
+        out_shape=slots,
+        in_specs=[SMEM, SMEM, VMEM, VMEM],
         out_specs=VMEM,
         name="mirror",
-    )(blocks, partner, sites, onchip(shifted), onchip(direct))
-    incoming = lax.all_to_all(outgoing, axes, split_axis=0, concat_axis=0, tiled=True)
+    )(blocks, partner, sites, onchip(shifted))
+    mirror = exchange(mirror)
     polar = pl.pallas_call(
         functools.partial(convolve_kernel, 8),
         out_shape=pltpu.VMEM((energies * ROWS, LANES), jnp.bfloat16),
-        in_specs=[VMEM],
+        in_specs=[VMEM, VMEM],
         out_specs=VMEM,
-        scratch_shapes=[pltpu.VMEM((energies, ROWS, LANES), jnp.float32)] * 2,
+        scratch_shapes=[pltpu.VMEM((energies, ROWS, LANES), jnp.float32)],
         name="convolve",
-    )(onchip(incoming))
-    returned = lax.all_to_all(
-        polar.reshape(energies, ROWS, LANES), axes, split_axis=0, concat_axis=0, tiled=True
-    )
+    )(onchip(direct), onchip(mirror))
+    returned = exchange(polar.reshape(energies, ROWS, LANES))
     result = pl.pallas_call(
         screen_kernel,
         out_shape=jax.ShapeDtypeStruct(couplings.shape, jnp.bfloat16),

time: 68.5 us -> 80.6 us (1.18)
  blocking collectives: 39.9 us -> 15.2 us
  starting transfers between devices: 14.2 us -> 35.2 us
  waiting for transfers between devices: 7.45 us -> 21.9 us
  Pallas kernels: 4.59 us -> 5.92 us
    all_to_all x2 -> x1, blocking collectives: 39.9 us -> 15.2 us  [exchange(): return lax.all_to_all(value, axes, split_axis=0, concat_axis=0, tiled=True)]
    all_to_all x0 -> x2, starting transfers between devices: none -> 20.9 us  [exchange(): return lax.all_to_all(value, axes, split_axis=0, concat_axis=0, tiled=True)]
    all_to_all x0 -> x2, waiting for transfers between devices: none -> 11.4 us  [exchange(): return lax.all_to_all(value, axes, split_axis=0, concat_axis=0, tiled=True)]
    ppermute x1, waiting for transfers between devices: 7.45 us -> 10.5 us  [per_device(): lax.ppermute(couplings, 'pair', [(i, (i + pairs // 2) % pairs) for i in r...]
    pallas_call x2 -> x3, Pallas kernels: 2.22 us -> 3.56 us  [the longest x1 1.79 us: per_device(): pl.pallas_call(mirror_kernel, out_shape=slots, in_specs=[SMEM, SMEM, VMEM...]
  transfers between devices with their start and end apart: 1 -> 3, of which waited for: 1 -> 2; matrix products, arithmetic and copies ran while one was open for 0% -> 0% of each run, Pallas kernels for 2% -> 2%
where the time goes in v4:
time: 80.6 us; the launch traced here: 80.2 us
  starting transfers between devices  35.2 us (44%)
  waiting for transfers between devices  21.9 us (27%)
  blocking collectives  15.2 us (19%)
  Pallas kernels  5.92 us (7%)
  local copies, waits for them, and re-layouts  1.95 us (2%)
    all_to_all x2, starting transfers between devices, exchange(): return lax.all_to_all(value, axes, split_axis=0, concat_axis=0, tiled=True)  20.9 us
    all_to_all x1, blocking collectives, exchange(): return lax.all_to_all(value, axes, split_axis=0, concat_axis=0, tiled=True)  15.2 us
    ppermute x1, starting transfers between devices, per_device(): lax.ppermute(couplings, 'pair', [(i, (i + pairs // 2) % pairs) for i in r...  14.2 us
    all_to_all x2, waiting for transfers between devices, exchange(): return lax.all_to_all(value, axes, split_axis=0, concat_axis=0, tiled=True)  11.4 us
    ppermute x1, waiting for transfers between devices, per_device(): lax.ppermute(couplings, 'pair', [(i, (i + pairs // 2) % pairs) for i in r...  10.5 us
    unnamed x6, local copies, waits for them, and re-layouts  1.95 us
    pallas_call x1, Pallas kernels, per_device(): pl.pallas_call(mirror_kernel, out_shape=slots, in_specs=[SMEM, SMEM, VMEM...  1.79 us
    pallas_call x1, Pallas kernels, per_device(): pl.pallas_call(screen_kernel, out_shape=jax.ShapeDtypeStruct(couplings.sh...  1.77 us
  transfers between devices with their start and end apart: 3, of which 2 were waited for; matrix products, arithmetic and copies ran while one was open for 0% of the time, Pallas kernels for 2%

profile of v4, /device:TPU:64, one launch (start us, length us, event | category | flops | bytes accessed | tf_op | source)
XLA Modules:
  0.0 80.2 jit_solution(10047686286722583445)
XLA Ops:
  0.0 0.0 copy-start
  0.0 1.0 %copy-done = bf16[6,1,160,160]{3,2,1,0:T(8,128)(2,1)S(1)} copy-done((bf16[6,1,160,160]{3,2,1,0:T(8,128)(2,1)S(1)}, bf16[6,1,160,160]{3,2,1,0:T(8,128)(2,1)}, u32[]{:S(2)}) %copy-start) | copy-done | bytes 307224
  1.0 0.0 copy-start.2
  1.0 0.9 %copy-done.2 = bf16[2,160,160]{2,1,0:T(8,128)(2,1)S(1)} copy-done((bf16[2,160,160]{2,1,0:T(8,128)(2,1)S(1)}, bf16[2,160,160]{2,1,0:T(8,128)(2,1)}, u32[]{:S(2)}) %copy-start.2) | copy-done | bytes 102424
  1.9 1.8 %direct.1 = bf16[64,8,128]{2,1,0:T(8,128)(2,1)} custom-call(s32[2,2]{1,0:T(2,128)} %blocks.5, bf16[6,160,160]{2,1,0:T(8,128)(2,1)S(1)} %bitcast.6, bf16[2,160,160]{2,1,0:T(8,128)(2,1)S(1)} %copy-done.2), custom_call_target="tpu_custom_call" | custom-call | tf_op jit(solution)/shard_map/direct/pallas_call | solution.py:131
  3.7 10.6 %all-to-all-start = ((bf16[64,8,128]{2,1,0:T(8,128)(2,1)}), bf16[64,8,128]{2,1,0:T(8,128)(2,1)S(1)}, u32[]{:S(2)}, u32[]{:S(2)}) async-start(bf16[64,8,128]{2,1,0:T(8,128)(2,1)} %direct.1), calls=%async_computation | async-start | bytes 262144 | tf_op jit(solution)/shard_map/all_to_all | solution.py:124
  14.3 14.2 %collective-permute-start = (bf16[2,160,160]{2,1,0:T(8,128)(2,1)S(1)}, bf16[2,160,160]{2,1,0:T(8,128)(2,1)S(1)}, u32[]{:S(2)}, u32[]{:S(2)}) collective-permute-start(bf16[2,160,160]{2,1,0:T(8,128)(2,1)S(1)} %copy-done.2), channel_id=1, source_target_pairs={{0,12},{2,14},{4,16},{6,18},{8,20},{10,22},{12,0},{14,2},{16,4},{1... | collective-permute-start | bytes 307208 | tf_op jit(solution)/shard_map/ppermute | solution.py:127
  28.5 10.5 %collective-permute-done.shifted = bf16[2,160,160]{2,1,0:T(8,128)(2,1)S(1)} collective-permute-done((bf16[2,160,160]{2,1,0:T(8,128)(2,1)S(1)}, bf16[2,160,160]{2,1,0:T(8,128)(2,1)S(1)}, u32[]{:S(2)}, u32[]{:S(2)}) %collective-permute-start) | collective-permute-done | bytes 102432 | tf_op jit(solution)/shard_map/ppermute | solution.py:127
  39.0 1.8 %mirror.1 = bf16[64,8,128]{2,1,0:T(8,128)(2,1)} custom-call(s32[2,2]{1,0:T(2,128)} %blocks.5, s32[2]{0:T(128)} %partner.1, bf16[6,160,160]{2,1,0:T(8,128)(2,1)S(1)} %bitcast.7, bf16[2,160,160]{2,1,0:T(8,128)(2,1)S(1)} %collective-permute-done.shifted), custom_call_target="tpu_custom_call" | custom-call | tf_op jit(solution)/shard_map/mirror/pallas_call | solution.py:146
  40.8 0.0 all-to-all-done.value
  40.8 10.3 %all-to-all-start.1 = ((bf16[64,8,128]{2,1,0:T(8,128)(2,1)}), bf16[64,8,128]{2,1,0:T(8,128)(2,1)S(1)}, u32[]{:S(2)}, u32[]{:S(2)}) async-start(bf16[64,8,128]{2,1,0:T(8,128)(2,1)} %mirror.1), calls=%async_computation.1 | async-start | bytes 262144 | tf_op jit(solution)/shard_map/all_to_all | solution.py:124
  51.2 0.0 copy-start.1
  51.2 11.4 %all-to-all-done.1.mirror = bf16[64,8,128]{2,1,0:T(8,128)(2,1)S(1)} async-done(((bf16[64,8,128]{2,1,0:T(8,128)(2,1)}), bf16[64,8,128]{2,1,0:T(8,128)(2,1)S(1)}, u32[]{:S(2)}, u32[]{:S(2)}) %all-to-all-start.1) | async-done | bytes 131104 | tf_op jit(solution)/shard_map/all_to_all | solution.py:124
  62.6 0.6 convolve.1
  63.2 15.2 %all_to_all.15 = bf16[64,8,128]{2,1,0:T(8,128)(2,1)S(1)} all-to-all(bf16[64,8,128]{2,1,0:T(8,128)(2,1)S(1)} %bitcast.9), channel_id=1, replica_groups=mesh['wide'=32,'pair'=12,'sub'=2] {'wide','sub'}, dimensions={0} | all-to-all | bytes 262144 | tf_op jit(solution)/shard_map/all_to_all | solution.py:124
  78.4 0.0 copy-done.1
  78.4 1.8 %screen.1 = bf16[2,160,160]{2,1,0:T(8,128)(2,1)} custom-call(s32[2,2]{1,0:T(2,128)} %blocks.5, bf16[6,160,160]{2,1,0:T(8,128)(2,1)S(1)} %bitcast.8, bf16[512,128]{1,0:T(8,128)(2,1)S(1)} %bitcast.10), custom_call_target="tpu_custom_call" | custom-call | tf_op jit(solution)/shard_map/screen/pallas_call | solution.py:163
  (1 shorter events, 0.0 us)
Async XLA Ops:
  0.0 1.0 %copy-start = (bf16[6,1,160,160]{3,2,1,0:T(8,128)(2,1)S(1)}, bf16[6,1,160,160]{3,2,1,0:T(8,128)(2,1)}, u32[]{:S(2)}) copy-start(bf16[6,1,160,160]{3,2,1,0:T(8,128)(2,1)} %param.4) | copy-start | bytes 921604
  1.0 0.9 %copy-start.2 = (bf16[2,160,160]{2,1,0:T(8,128)(2,1)S(1)}, bf16[2,160,160]{2,1,0:T(8,128)(2,1)}, u32[]{:S(2)}) copy-start(bf16[2,160,160]{2,1,0:T(8,128)(2,1)} %couplings.1) | copy-start | bytes 307204
  3.7 37.1 %all-to-all-start = ((bf16[64,8,128]{2,1,0:T(8,128)(2,1)}), bf16[64,8,128]{2,1,0:T(8,128)(2,1)S(1)}, u32[]{:S(2)}, u32[]{:S(2)}) async-start(bf16[64,8,128]{2,1,0:T(8,128)(2,1)} %direct.1), calls=%async_computation | async-start | bytes 262144 | tf_op jit(solution)/shard_map/all_to_all | solution.py:124
  14.3 24.7 %collective-permute-start = (bf16[2,160,160]{2,1,0:T(8,128)(2,1)S(1)}, bf16[2,160,160]{2,1,0:T(8,128)(2,1)S(1)}, u32[]{:S(2)}, u32[]{:S(2)}) collective-permute-start(bf16[2,160,160]{2,1,0:T(8,128)(2,1)S(1)} %copy-done.2), channel_id=1, source_target_pairs={{0,12},{2,14},{4,16},{6,18},{8,20},{10,22},{12,0},{14,2},{16,4},{1... | collective-permute-start | bytes 307208 | tf_op jit(solution)/shard_map/ppermute | solution.py:127
  40.8 21.8 %all-to-all-start.1 = ((bf16[64,8,128]{2,1,0:T(8,128)(2,1)}), bf16[64,8,128]{2,1,0:T(8,128)(2,1)S(1)}, u32[]{:S(2)}, u32[]{:S(2)}) async-start(bf16[64,8,128]{2,1,0:T(8,128)(2,1)} %mirror.1), calls=%async_computation.1 | async-start | bytes 262144 | tf_op jit(solution)/shard_map/all_to_all | solution.py:124
  51.2 27.2 %copy-start.1 = (bf16[6,1,160,160]{3,2,1,0:T(8,128)(2,1)S(1)}, bf16[6,1,160,160]{3,2,1,0:T(8,128)(2,1)}, u32[]{:S(2)}) copy-start(bf16[6,1,160,160]{3,2,1,0:T(8,128)(2,1)} %param.4) | copy-start | bytes 921604

commit v5 on v2

--- a/solution.py
+++ b/solution.py
@@ -37,23 +37,40 @@
     return jnp.concatenate([first[:, :LANES], second[:, :LANES], rest], axis=0)
 
 
-def direct_kernel(blocks, orbitals, couplings, out):
+def unpack(packed, order, b):
+    half = order // 2
+    width = order - LANES
+    rest = packed[2 * order : 2 * order + half, :]
+    at = 2 * b * width
+    tail = jnp.concatenate(
+        [rest[:, at : at + width], rest[:, at + width : at + 2 * width]], axis=0
+    )
+    return jnp.concatenate([packed[b * order : (b + 1) * order, :], tail], axis=1)
+
+
+def send_kernel(partner, couplings, out):
+    first = lax.rem(partner[0], 2)
+    out[...] = pack(couplings[first], couplings[1 - first])
+
+
+def direct_kernel(blocks, orbitals, couplings, out, factors):
     results = []
     for b in range(2):
         left = orbitals[blocks[b, 0]]
         right = orbitals[blocks[b, 1]]
+        factors[2 * b] = left
+        factors[2 * b + 1] = right
         inner = matmul(left, couplings[b]).astype(jnp.bfloat16)
         results.append(matmul_t(inner, right))
     out[...] = pack(*results).astype(jnp.bfloat16)
 
 
-def mirror_kernel(blocks, partner, orbitals, shifted, direct, out):
+def mirror_kernel(factors, shifted, direct, out):
     results = []
     for b in range(2):
-        left = orbitals[blocks[b, 0]]
-        right = orbitals[blocks[b, 1]]
-        across = matmul(right, shifted[lax.rem(partner[b], 2)]).astype(jnp.bfloat16)
-        results.append(matmul_t(left, across))
+        coupling = unpack(shifted, factors.shape[1], b)
+        across = matmul(factors[2 * b + 1], coupling).astype(jnp.bfloat16)
+        results.append(matmul_t(factors[2 * b], across))
     mirror = pack(*results)
     used = direct.shape[0] // ROWS
     both = jnp.concatenate(
@@ -93,21 +110,17 @@
             out[pl.ds((e0 + de) * ROWS, 2 * ROWS), :] = pair.astype(jnp.bfloat16)
 
 
-def screen_kernel(blocks, orbitals, packed, out):
-    order = out.shape[1]
-    half = order // 2
-    rest = packed[2 * order : 2 * order + half, :]
-    width = order - LANES
+def screen_kernel(factors, packed, out, held, sems):
+    copies = []
     for b in range(2):
-        left = orbitals[blocks[b, 0]]
-        right = orbitals[blocks[b, 1]]
-        at = 2 * b * width
-        tail = jnp.concatenate(
-            [rest[:, at : at + width], rest[:, at + width : at + 2 * width]], axis=0
-        )
-        polar = jnp.concatenate([packed[b * order : (b + 1) * order, :], tail], axis=1)
-        screened = matmul(left, polar).astype(jnp.bfloat16)
-        out[b] = matmul_t(screened, right).astype(jnp.bfloat16)
+        polar = unpack(packed, held.shape[1], b)
+        screened = matmul(factors[2 * b], polar).astype(jnp.bfloat16)
+        held[b] = matmul_t(screened, factors[2 * b + 1]).astype(jnp.bfloat16)
+        copy = pltpu.make_async_copy(held.at[b], out.at[b], sems.at[b])
+        copy.start()
+        copies.append(copy)
+    for copy in copies:
+        copy.wait()
 
 
 def onchip(value):
@@ -120,25 +133,32 @@
     pairs = lax.axis_size("pair")
     order = couplings.shape[1]
     packed_rows = 2 * order * order // LANES
+    packed = pltpu.VMEM((packed_rows, LANES), jnp.bfloat16)
+    leaving = pl.pallas_call(
+        send_kernel,
+        out_shape=packed,
+        in_specs=[SMEM, VMEM],
+        out_specs=VMEM,
+        name="send",
+    )(partner, couplings)
     shifted = lax.ppermute(
-        couplings, "pair", [(i, (i + pairs // 2) % pairs) for i in range(pairs)]
-    )
-    sites = onchip(orbitals.reshape(orbitals.shape[0], order, order))
-    here = onchip(couplings)
-    direct = pl.pallas_call(
+        leaving, "pair", [(i, (i + pairs // 2) % pairs) for i in range(pairs)]
+    )
+    sites = orbitals.reshape(orbitals.shape[0], order, order)
+    direct, factors = pl.pallas_call(
         direct_kernel,
-        out_shape=pltpu.VMEM((packed_rows, LANES), jnp.bfloat16),
+        out_shape=[packed, pltpu.VMEM((4, order, order), jnp.bfloat16)],
         in_specs=[SMEM, VMEM, VMEM],
-        out_specs=VMEM,
+        out_specs=[VMEM, VMEM],
         name="direct",
-    )(blocks, sites, here)
+    )(blocks, onchip(sites), onchip(couplings))
     outgoing = pl.pallas_call(
         mirror_kernel,
         out_shape=pltpu.VMEM((energies, 2 * ROWS, LANES), jnp.bfloat16),
-        in_specs=[SMEM, SMEM, VMEM, VMEM, VMEM],
+        in_specs=[VMEM, VMEM, VMEM],
         out_specs=VMEM,
         name="mirror",
-    )(blocks, partner, sites, onchip(shifted), onchip(direct))
+    )(onchip(factors), onchip(shifted), onchip(direct))
     incoming = lax.all_to_all(outgoing, axes, split_axis=0, concat_axis=0, tiled=True)
     polar = pl.pallas_call(
         functools.partial(convolve_kernel, 8),
@@ -154,10 +174,14 @@
     result = pl.pallas_call(
         screen_kernel,
         out_shape=jax.ShapeDtypeStruct(couplings.shape, jnp.bfloat16),
-        in_specs=[SMEM, VMEM, VMEM],
-        out_specs=VMEM,
+        in_specs=[VMEM, VMEM],
+        out_specs=pl.BlockSpec(memory_space=pl.ANY),
+        scratch_shapes=[
+            pltpu.VMEM(couplings.shape, jnp.bfloat16),
+            pltpu.SemaphoreType.DMA((2,)),
+        ],
         name="screen",
-    )(blocks, sites, onchip(returned.reshape(energies * ROWS, LANES)))
+    )(onchip(factors), onchip(returned.reshape(energies * ROWS, LANES)))
     return result.reshape(couplings.shape[0], 1, order, order)
 
 

time: 68.5 us -> 65 us (0.949)
  waiting for transfers between devices: 7.45 us -> 5.22 us
  local copies, waits for them, and re-layouts: 1.95 us -> 1.03 us
    ppermute x1, waiting for transfers between devices: 7.45 us -> 5.22 us  [per_device(): lax.ppermute(leaving, 'pair', [(i, (i + pairs // 2) % pairs) for i in ran...]
    pallas_call x1 -> x2, Pallas kernels: 1.09 us -> 2.18 us  [the longest x1 1.09 us: per_device(): pl.pallas_call(direct_kernel, out_shape=[packed, pltpu.VMEM((4, order, or...]
    unnamed x6 -> x4, local copies, waits for them, and re-layouts: 1.95 us -> 1.03 us
    pallas_call x1, Pallas kernels: 1.77 us -> 1.08 us  [per_device(): pl.pallas_call(screen_kernel, out_shape=jax.ShapeDtypeStruct(couplings.sh...]
where the time goes in v5:
time: 65 us; the launch traced here: 64.7 us
  blocking collectives  39.8 us (61%)
  starting transfers between devices  14.2 us (22%)
  waiting for transfers between devices  5.22 us (8%)
  Pallas kernels  4.38 us (7%)
  local copies, waits for them, and re-layouts  1.03 us (2%)
    all_to_all x1, blocking collectives, per_device(): lax.all_to_all(outgoing, axes, split_axis=0, concat_axis=0, tiled=True)  24.6 us
    all_to_all x1, blocking collectives, per_device(): lax.all_to_all(polar.reshape(energies, ROWS, LANES), axes, split_axis=0,...  15.2 us
    ppermute x1, starting transfers between devices, per_device(): lax.ppermute(leaving, 'pair', [(i, (i + pairs // 2) % pairs) for i in ran...  14.2 us
    ppermute x1, waiting for transfers between devices, per_device(): lax.ppermute(leaving, 'pair', [(i, (i + pairs // 2) % pairs) for i in ran...  5.22 us
  transfers between devices with their start and end apart: 1, of which 1 were waited for; matrix products, arithmetic and copies ran while one was open for 0% of the time, Pallas kernels for 2%

profile of v5, /device:TPU:64, one launch (start us, length us, event | category | flops | bytes accessed | tf_op | source)
XLA Modules:
  0.0 64.7 jit_solution(14142651656695192427)
XLA Ops:
  0.0 0.0 copy-start
  0.0 1.1 %send.1 = bf16[400,128]{1,0:T(8,128)(2,1)S(1)} custom-call(s32[2]{0:T(128)} %partner.1, bf16[2,160,160]{2,1,0:T(8,128)(2,1)} %couplings.3), custom_call_target="tpu_custom_call" | custom-call | tf_op jit(solution)/shard_map/send/pallas_call | solution.py:137
  1.1 14.2 %collective-permute-start = (bf16[400,128]{1,0:T(8,128)(2,1)S(1)}, bf16[400,128]{1,0:T(8,128)(2,1)S(1)}, u32[]{:S(2)}, u32[]{:S(2)}) collective-permute-start(bf16[400,128]{1,0:T(8,128)(2,1)S(1)} %send.1), channel_id=1, source_target_pairs={{0,12},{2,14},{4,16},{6,18},{8,20},{10,22},{12,0},{14,2},{16,4},{1... | collective-permute-start | bytes 307208 | tf_op jit(solution)/shard_map/ppermute | solution.py:144
  15.3 0.0 copy-done
  15.4 0.0 copy-start.1
  15.4 1.0 %copy-done.1 = bf16[6,1,160,160]{3,2,1,0:T(8,128)(2,1)S(1)} copy-done((bf16[6,1,160,160]{3,2,1,0:T(8,128)(2,1)S(1)}, bf16[6,1,160,160]{3,2,1,0:T(8,128)(2,1)}, u32[]{:S(2)}) %copy-start.1) | copy-done | bytes 307224
  16.4 1.1 %direct.1 = (bf16[400,128]{1,0:T(8,128)(2,1)S(1)}, bf16[4,160,160]{2,1,0:T(8,128)(2,1)S(1)}) custom-call(s32[2,2]{1,0:T(2,128)} %blocks.1, bf16[6,160,160]{2,1,0:T(8,128)(2,1)S(1)} %bitcast.8, bf16[2,160,160]{2,1,0:T(8,128)(2,1)S(1)} %copy-done), custom_call_target="tpu_custom_call" | custom-call | tf_op jit(solution)/shard_map/direct/pallas_call | solution.py:148
  17.5 5.2 %collective-permute-done.shifted = bf16[400,128]{1,0:T(8,128)(2,1)S(1)} collective-permute-done((bf16[400,128]{1,0:T(8,128)(2,1)S(1)}, bf16[400,128]{1,0:T(8,128)(2,1)S(1)}, u32[]{:S(2)}, u32[]{:S(2)}) %collective-permute-start) | collective-permute-done | bytes 102432 | tf_op jit(solution)/shard_map/ppermute | solution.py:144
  22.7 0.5 mirror.1
  23.2 24.6 %all_to_all.10.incoming = bf16[64,16,128]{2,1,0:T(8,128)(2,1)S(1)} all-to-all(bf16[64,16,128]{2,1,0:T(8,128)(2,1)S(1)} %mirror.1), channel_id=1, replica_groups=mesh['wide'=32,'pair'=12,'sub'=2] {'wide','sub'}, dimensions={0} | all-to-all | bytes 524288 | tf_op jit(solution)/shard_map/all_to_all | solution.py:162
  47.8 0.6 convolve.1
  48.4 15.2 %all_to_all.11 = bf16[64,8,128]{2,1,0:T(8,128)(2,1)S(1)} all-to-all(bf16[64,8,128]{2,1,0:T(8,128)(2,1)S(1)} %bitcast.7), channel_id=1, replica_groups=mesh['wide'=32,'pair'=12,'sub'=2] {'wide','sub'}, dimensions={0} | all-to-all | bytes 262144 | tf_op jit(solution)/shard_map/all_to_all | solution.py:171
  63.6 1.1 %screen.1 = bf16[2,160,160]{2,1,0:T(8,128)(2,1)} custom-call(bf16[4,160,160]{2,1,0:T(8,128)(2,1)S(1)} %get-tuple-element.7.factors, bf16[512,128]{1,0:T(8,128)(2,1)S(1)} %bitcast.6), custom_call_target="tpu_custom_call" | custom-call | tf_op jit(solution)/shard_map/screen/pallas_call | solution.py:174
Async XLA Ops:
  0.0 15.3 %copy-start = (bf16[2,160,160]{2,1,0:T(8,128)(2,1)S(1)}, bf16[2,160,160]{2,1,0:T(8,128)(2,1)}, u32[]{:S(2)}) copy-start(bf16[2,160,160]{2,1,0:T(8,128)(2,1)} %couplings.3) | copy-start | bytes 307204
  1.1 21.6 %collective-permute-start = (bf16[400,128]{1,0:T(8,128)(2,1)S(1)}, bf16[400,128]{1,0:T(8,128)(2,1)S(1)}, u32[]{:S(2)}, u32[]{:S(2)}) collective-permute-start(bf16[400,128]{1,0:T(8,128)(2,1)S(1)} %send.1), channel_id=1, source_target_pairs={{0,12},{2,14},{4,16},{6,18},{8,20},{10,22},{12,0},{14,2},{16,4},{1... | collective-permute-start | bytes 307208 | tf_op jit(solution)/shard_map/ppermute | solution.py:144
  15.4 1.0 %copy-start.1 = (bf16[6,1,160,160]{3,2,1,0:T(8,128)(2,1)S(1)}, bf16[6,1,160,160]{3,2,1,0:T(8,128)(2,1)}, u32[]{:S(2)}) copy-start(bf16[6,1,160,160]{3,2,1,0:T(8,128)(2,1)} %param.4) | copy-start | bytes 921604

commit v6 on v5

--- a/solution.py
+++ b/solution.py
@@ -48,30 +48,46 @@
     return jnp.concatenate([packed[b * order : (b + 1) * order, :], tail], axis=1)
 
 
-def send_kernel(partner, couplings, out):
+def send_kernel(couplings, out):
+    out[...] = pack(couplings[0], couplings[1])
+
+
+def direct_kernel(blocks, partner, orbitals, couplings, out, factors, arriving, crossed):
     first = lax.rem(partner[0], 2)
-    out[...] = pack(couplings[first], couplings[1 - first])
-
-
-def direct_kernel(blocks, orbitals, couplings, out, factors):
     results = []
     for b in range(2):
         left = orbitals[blocks[b, 0]]
         right = orbitals[blocks[b, 1]]
-        factors[2 * b] = left
-        factors[2 * b + 1] = right
+        slot = first if b == 0 else 1 - first
+        for side, factor in enumerate((left, right)):
+            factors[2 * b + side] = factor
+            arriving[2 * slot + side] = factor
         inner = matmul(left, couplings[b]).astype(jnp.bfloat16)
         results.append(matmul_t(inner, right))
     out[...] = pack(*results).astype(jnp.bfloat16)
-
-
-def mirror_kernel(factors, shifted, direct, out):
+    crossed[...] = jnp.full(crossed.shape, first, jnp.int32)
+
+
+def mirror_kernel(factors, crossed, shifted, direct, out):
     results = []
     for b in range(2):
         coupling = unpack(shifted, factors.shape[1], b)
         across = matmul(factors[2 * b + 1], coupling).astype(jnp.bfloat16)
         results.append(matmul_t(factors[2 * b], across))
-    mirror = pack(*results)
+    arrived = pack(*results)
+    order = factors.shape[1]
+    swap = jnp.broadcast_to(crossed[0:1, :], arrived.shape) > 0
+    half = (order - LANES) * 2
+    rest = arrived[2 * order :]
+    turned = jnp.concatenate(
+        [
+            arrived[order : 2 * order],
+            arrived[:order],
+            jnp.concatenate([rest[:, half:], rest[:, :half]], axis=1),
+        ],
+        axis=0,
+    )
+    mirror = jnp.where(swap, turned, arrived)
     used = direct.shape[0] // ROWS
     both = jnp.concatenate(
         [
@@ -137,28 +153,29 @@
     leaving = pl.pallas_call(
         send_kernel,
         out_shape=packed,
-        in_specs=[SMEM, VMEM],
+        in_specs=[VMEM],
         out_specs=VMEM,
         name="send",
-    )(partner, couplings)
+    )(couplings)
     shifted = lax.ppermute(
         leaving, "pair", [(i, (i + pairs // 2) % pairs) for i in range(pairs)]
     )
     sites = orbitals.reshape(orbitals.shape[0], order, order)
-    direct, factors = pl.pallas_call(
+    chosen = pltpu.VMEM((4, order, order), jnp.bfloat16)
+    direct, factors, arriving, crossed = pl.pallas_call(
         direct_kernel,
-        out_shape=[packed, pltpu.VMEM((4, order, order), jnp.bfloat16)],
-        in_specs=[SMEM, VMEM, VMEM],
-        out_specs=[VMEM, VMEM],
+        out_shape=[packed, chosen, chosen, pltpu.VMEM((ROWS, LANES), jnp.int32)],
+        in_specs=[SMEM, SMEM, VMEM, VMEM],
+        out_specs=[VMEM] * 4,
         name="direct",
-    )(blocks, onchip(sites), onchip(couplings))
+    )(blocks, partner, onchip(sites), onchip(couplings))
     outgoing = pl.pallas_call(
         mirror_kernel,
         out_shape=pltpu.VMEM((energies, 2 * ROWS, LANES), jnp.bfloat16),
-        in_specs=[VMEM, VMEM, VMEM],
+        in_specs=[VMEM] * 4,
         out_specs=VMEM,
         name="mirror",
-    )(onchip(factors), onchip(shifted), onchip(direct))
+    )(onchip(arriving), onchip(crossed), onchip(shifted), onchip(direct))
     incoming = lax.all_to_all(outgoing, axes, split_axis=0, concat_axis=0, tiled=True)
     polar = pl.pallas_call(
         functools.partial(convolve_kernel, 8),

time: 65 us -> 65 us (level)
  no operation moved by 1% of the time
where the time goes in v6:
time: 65 us; the launch traced here: 64.7 us
  blocking collectives  39.8 us (61%)
  starting transfers between devices  14.2 us (22%)
  waiting for transfers between devices  5.22 us (8%)
  Pallas kernels  4.44 us (7%)
  local copies, waits for them, and re-layouts  1.03 us (2%)
    all_to_all x1, blocking collectives, per_device(): lax.all_to_all(outgoing, axes, split_axis=0, concat_axis=0, tiled=True)  24.6 us
    all_to_all x1, blocking collectives, per_device(): lax.all_to_all(polar.reshape(energies, ROWS, LANES), axes, split_axis=0,...  15.2 us
    ppermute x1, starting transfers between devices, per_device(): lax.ppermute(leaving, 'pair', [(i, (i + pairs // 2) % pairs) for i in ran...  14.2 us
    ppermute x1, waiting for transfers between devices, per_device(): lax.ppermute(leaving, 'pair', [(i, (i + pairs // 2) % pairs) for i in ran...  5.22 us
  transfers between devices with their start and end apart: 1, of which 1 were waited for; matrix products, arithmetic and copies ran while one was open for 0% of the time, Pallas kernels for 2%

profile of v6, /device:TPU:64, one launch (start us, length us, event | category | flops | bytes accessed | tf_op | source)
XLA Modules:
  0.0 64.7 jit_solution(4813024399475560619)
XLA Ops:
  0.0 0.0 copy-start
  0.0 1.1 %send.1 = bf16[400,128]{1,0:T(8,128)(2,1)S(1)} custom-call(bf16[2,160,160]{2,1,0:T(8,128)(2,1)} %couplings.3), custom_call_target="tpu_custom_call" | custom-call | tf_op jit(solution)/shard_map/send/pallas_call | solution.py:153
  1.1 14.2 %collective-permute-start = (bf16[400,128]{1,0:T(8,128)(2,1)S(1)}, bf16[400,128]{1,0:T(8,128)(2,1)S(1)}, u32[]{:S(2)}, u32[]{:S(2)}) collective-permute-start(bf16[400,128]{1,0:T(8,128)(2,1)S(1)} %send.1), channel_id=1, source_target_pairs={{0,12},{2,14},{4,16},{6,18},{8,20},{10,22},{12,0},{14,2},{16,4},{1... | collective-permute-start | bytes 307208 | tf_op jit(solution)/shard_map/ppermute | solution.py:160
  15.3 0.0 copy-done
  15.3 0.0 copy-start.1
  15.3 1.0 %copy-done.1 = bf16[6,1,160,160]{3,2,1,0:T(8,128)(2,1)S(1)} copy-done((bf16[6,1,160,160]{3,2,1,0:T(8,128)(2,1)S(1)}, bf16[6,1,160,160]{3,2,1,0:T(8,128)(2,1)}, u32[]{:S(2)}) %copy-start.1) | copy-done | bytes 307224
  16.4 1.1 %direct.1 = (bf16[400,128]{1,0:T(8,128)(2,1)S(1)}, bf16[4,160,160]{2,1,0:T(8,128)(2,1)S(1)}, bf16[4,160,160]{2,1,0:T(8,128)(2,1)S(1)}, s32[8,128]{1,0:T(8,128)S(1)}) custom-call(s32[2,2]{1,0:T(2,128)} %blocks.1, s32[2]{0:T(128)} %partner.1, bf16[6,160,160]{2,1,0:T(8,128)(2,1)S(1)} %bitcast.8, bf16[2,160,160]{2,1,0:T(8,128)(2,1)S(1)} %copy-done), custom_call_target="tpu_custom_call" | custom-call | tf_op jit(solution)/shard_map/direct/pallas_call | solution.py:165
  17.5 5.2 %collective-permute-done.shifted = bf16[400,128]{1,0:T(8,128)(2,1)S(1)} collective-permute-done((bf16[400,128]{1,0:T(8,128)(2,1)S(1)}, bf16[400,128]{1,0:T(8,128)(2,1)S(1)}, u32[]{:S(2)}, u32[]{:S(2)}) %collective-permute-start) | collective-permute-done | bytes 102432 | tf_op jit(solution)/shard_map/ppermute | solution.py:160
  22.7 0.6 mirror.1
  23.3 24.6 %all_to_all.10.incoming = bf16[64,16,128]{2,1,0:T(8,128)(2,1)S(1)} all-to-all(bf16[64,16,128]{2,1,0:T(8,128)(2,1)S(1)} %mirror.1), channel_id=1, replica_groups=mesh['wide'=32,'pair'=12,'sub'=2] {'wide','sub'}, dimensions={0} | all-to-all | bytes 524288 | tf_op jit(solution)/shard_map/all_to_all | solution.py:179
  47.9 0.6 convolve.1
  48.4 15.2 %all_to_all.11 = bf16[64,8,128]{2,1,0:T(8,128)(2,1)S(1)} all-to-all(bf16[64,8,128]{2,1,0:T(8,128)(2,1)S(1)} %bitcast.7), channel_id=1, replica_groups=mesh['wide'=32,'pair'=12,'sub'=2] {'wide','sub'}, dimensions={0} | all-to-all | bytes 262144 | tf_op jit(solution)/shard_map/all_to_all | solution.py:188
  63.7 1.1 %screen.1 = bf16[2,160,160]{2,1,0:T(8,128)(2,1)} custom-call(bf16[4,160,160]{2,1,0:T(8,128)(2,1)S(1)} %get-tuple-element.9.factors, bf16[512,128]{1,0:T(8,128)(2,1)S(1)} %bitcast.6), custom_call_target="tpu_custom_call" | custom-call | tf_op jit(solution)/shard_map/screen/pallas_call | solution.py:191
Async XLA Ops:
  0.0 15.3 %copy-start = (bf16[2,160,160]{2,1,0:T(8,128)(2,1)S(1)}, bf16[2,160,160]{2,1,0:T(8,128)(2,1)}, u32[]{:S(2)}) copy-start(bf16[2,160,160]{2,1,0:T(8,128)(2,1)} %couplings.3) | copy-start | bytes 307204
  1.1 21.6 %collective-permute-start = (bf16[400,128]{1,0:T(8,128)(2,1)S(1)}, bf16[400,128]{1,0:T(8,128)(2,1)S(1)}, u32[]{:S(2)}, u32[]{:S(2)}) collective-permute-start(bf16[400,128]{1,0:T(8,128)(2,1)S(1)} %send.1), channel_id=1, source_target_pairs={{0,12},{2,14},{4,16},{6,18},{8,20},{10,22},{12,0},{14,2},{16,4},{1... | collective-permute-start | bytes 307208 | tf_op jit(solution)/shard_map/ppermute | solution.py:160
  15.3 1.0 %copy-start.1 = (bf16[6,1,160,160]{3,2,1,0:T(8,128)(2,1)S(1)}, bf16[6,1,160,160]{3,2,1,0:T(8,128)(2,1)}, u32[]{:S(2)}) copy-start(bf16[6,1,160,160]{3,2,1,0:T(8,128)(2,1)} %param.4) | copy-start | bytes 921604
